TPU v7x, 512 devices: a whole 4x8x8 slice. The times are simulated.
512 devices in a mesh: doc: 16 (over y, x_hi), seq: 32 (over z, x_lo, core).
Axes of the slice: x: 4 (x_hi: 2, x_lo: 2; x = x_hi * 2 + x_lo), y: 8, z: 8, core: 2. Of those that a mesh axis runs over, the one named last changes fastest.
Arguments:
- enc_query: bfloat16 [16, 4096, 2048], P('doc', 'seq'), may hold values from -40 to 40
- enc_key: bfloat16 [16, 4096, 2048], P('doc', 'seq'), may hold values from -16 to 16
- enc_value: bfloat16 [16, 4096, 2048], P('doc', 'seq'), may hold values from -6 to 6
- sum_query: bfloat16 [16, 512, 2048], P('doc', 'seq'), may hold values from -70 to 70
- doc_len: int32 [16], P('doc'), may hold values from 1024 to 4096, as said below
- w_memory: bfloat16 [2, 2048, 2048], P(None, None, 'doc'), may hold values from -0.26367188 to 0.26367188
Outputs:
- encoder_out: bfloat16 [16, 4096, 2048], P('doc', 'seq')
- summary_out: bfloat16 [16, 512, 2048], P('doc', 'seq')
Inputs may be any that keep to these rules, and one draw needn't show every extreme that they name: `doc_len`: at least one document has all 4096 tokens valid.
All inputs are finite; a program needn't handle non-finite values.
Results may differ from a plain program's by a relative error of at most 0.012.
Values may be sent and summed in bfloat16 or wider, within the bound.
A program may use at most 64 MiB of HBM per device.

v0:
```python
import math
import jax
import jax.numpy as jnp
from jax import lax
from jax.sharding import PartitionSpec as P

HEAD_DIM = 64


def attend_heads(queries, keys_all, values_all, length, head_dim):
    row_count = queries.shape[0]
    feature_width = queries.shape[1]
    head_count = feature_width // head_dim
    block_rows = math.gcd(row_count, 512)
    grouped = queries.reshape(row_count // block_rows, block_rows, head_count, head_dim)
    key_heads = keys_all.reshape(-1, head_count, head_dim)
    value_heads = values_all.reshape(-1, head_count, head_dim)
    key_valid = jnp.arange(key_heads.shape[0]) < length

    def one_block(query_block):
        scores = jnp.einsum(
            "qhd,khd->hqk", query_block, key_heads, preferred_element_type=jnp.float32
        ) * head_dim ** (-0.5)
        scores = jnp.where(key_valid[None, None, :], scores, -1e30)
        row_max = jnp.max(scores, axis=-1, keepdims=True)
        weights = jnp.exp(scores - row_max)
        denominator = jnp.sum(weights, axis=-1)
        weighted = jnp.einsum(
            "hqk,khd->qhd",
            weights.astype(jnp.bfloat16),
            value_heads,
            preferred_element_type=jnp.float32,
        )
        return (weighted / denominator.T[:, :, None]).astype(jnp.bfloat16)

    return lax.map(one_block, grouped).reshape(row_count, feature_width)


def shards(enc_query, enc_key, enc_value, sum_query, doc_len, w_memory):
    head_dim = HEAD_DIM
    length = doc_len[0]
    head_query, head_key, head_value = (
        lax.all_to_all(enc_query[0], "seq", split_axis=1, concat_axis=0, tiled=True),
        lax.all_to_all(enc_key[0], "seq", split_axis=1, concat_axis=0, tiled=True),
        lax.all_to_all(enc_value[0], "seq", split_axis=1, concat_axis=0, tiled=True),
    )
    context = attend_heads(head_query, head_key, head_value, length, head_dim)
    encoder_out = lax.all_to_all(context, "seq", split_axis=0, concat_axis=1, tiled=True)
    made = jnp.einsum(
        "btd,kdc->btkc",
        lax.all_gather(encoder_out[None], "doc", axis=0, tiled=True),
        w_memory,
        preferred_element_type=jnp.float32,
    )
    memory_rows = made.astype(jnp.bfloat16)
    memory_local = lax.all_to_all(
        lax.all_to_all(memory_rows, "doc", split_axis=0, concat_axis=3, tiled=True),
        "seq",
        split_axis=3,
        concat_axis=1,
        tiled=True,
    )
    memory_keys = memory_local[0, :, 0, :]
    memory_values = memory_local[0, :, 1, :]
    summary_heads = lax.all_to_all(sum_query[0], "seq", split_axis=1, concat_axis=0, tiled=True)
    answer = attend_heads(summary_heads, memory_keys, memory_values, length, head_dim)
    summary_out = lax.all_to_all(answer, "seq", split_axis=0, concat_axis=1, tiled=True)
    return (encoder_out[None], summary_out[None])


def solution(mesh):
    in_specs = (
        P("doc", "seq", None),
        P("doc", "seq", None),
        P("doc", "seq", None),
        P("doc", "seq", None),
        P("doc"),
        P(None, None, "doc"),
    )
    out_specs = (P("doc", "seq", None), P("doc", "seq", None))
    return jax.shard_map(shards, mesh=mesh, in_specs=in_specs, out_specs=out_specs, check_vma=False)
```

profile of v0, /device:TPU:1, one launch (start us, length us, event | category | flops | bytes accessed | tf_op | source)
XLA Modules:
  0.0 431.8 jit_solution(14560852746288561887)
XLA Ops:
  9.3 12.9 %all-to-all-start = ((bf16[128,32,64]{0,2,1:T(8,128)(2,1)}), bf16[128,32,64]{0,2,1:T(8,128)(2,1)S(1)}, u32[]{:S(2)}, u32[]{:S(2)}) async-start(bf16[128,32,64]{0,2,1:T(8,128)(2,1)} %bitcast), calls=%async_computation | async-start | bytes 1048576 | tf_op jit(solution)/shard_map/all_to_all | solution.py:43
  24.3 14.7 %all-to-all-done = bf16[128,32,64]{0,2,1:T(8,128)(2,1)S(1)} async-done(((bf16[128,32,64]{0,2,1:T(8,128)(2,1)}), bf16[128,32,64]{0,2,1:T(8,128)(2,1)S(1)}, u32[]{:S(2)}, u32[]{:S(2)}) %all-to-all-start) | async-done | bytes 524320 | tf_op jit(solution)/shard_map/all_to_all | solution.py:43
  38.9 5.1 %all-to-all-start.1 = ((bf16[128,32,64]{0,2,1:T(8,128)(2,1)}), bf16[128,32,64]{0,2,1:T(8,128)(2,1)S(1)}, u32[]{:S(2)}, u32[]{:S(2)}) async-start(bf16[128,32,64]{0,2,1:T(8,128)(2,1)} %bitcast.2), calls=%async_computation.1 | async-start | bytes 1048576 | tf_op jit(solution)/shard_map/all_to_all | solution.py:44
  46.1 15.0 %all-to-all-done.1 = bf16[128,32,64]{0,2,1:T(8,128)(2,1)S(1)} async-done(((bf16[128,32,64]{0,2,1:T(8,128)(2,1)}), bf16[128,32,64]{0,2,1:T(8,128)(2,1)S(1)}, u32[]{:S(2)}, u32[]{:S(2)}) %all-to-all-start.1) | async-done | bytes 524320 | tf_op jit(solution)/shard_map/all_to_all | solution.py:44
  61.1 4.8 %all-to-all-start.2 = ((bf16[128,32,64]{0,2,1:T(8,128)(2,1)}), bf16[128,32,64]{0,2,1:T(8,128)(2,1)S(1)}, u32[]{:S(2)}, u32[]{:S(2)}) async-start(bf16[128,32,64]{0,2,1:T(8,128)(2,1)} %bitcast.4), calls=%async_computation.2 | async-start | bytes 1048576 | tf_op jit(solution)/shard_map/all_to_all | solution.py:45
  68.2 14.8 %all-to-all-done.2 = bf16[128,32,64]{0,2,1:T(8,128)(2,1)S(1)} async-done(((bf16[128,32,64]{0,2,1:T(8,128)(2,1)}), bf16[128,32,64]{0,2,1:T(8,128)(2,1)S(1)}, u32[]{:S(2)}, u32[]{:S(2)}) %all-to-all-start.2) | async-done | bytes 524320 | tf_op jit(solution)/shard_map/all_to_all | solution.py:45
  83.6 60.9 %while.3 = (s32[]{:T(128)}, bf16[8,512,1,64]{1,3,2,0:T(8,128)(2,1)}, bf16[8,512,1,64]{1,3,2,0:T(8,128)(2,1)}, bf16[4096,1,64]{0,2,1:T(8,128)(2,1)S(1)}, bf16[409...) while((s32[]{:T(128)}, bf16[8,512,1,64]{1,3,2,0:T(8,128)(2,1)}, ...), condition=%wide.region_3.4_spmd.clone, body=%wide.region_0.3_spmd.clone.sunk | while | flops 560008192 | bytes 26373200 | solution.py:36
  88.7 2.5 fusion.68
  103.9 2.5 fusion.68
  111.5 2.5 fusion.68
  126.8 2.5 fusion.68
  142.0 2.5 fusion.68
  146.4 20.8 %all_to_all.132 = bf16[32,128,64]{1,2,0:T(8,128)(2,1)S(1)} all-to-all(bf16[32,128,64]{1,2,0:T(8,128)(2,1)S(1)} %copy.51), channel_id=1, replica_groups=mesh['doc'=16,'seq'=32] {'seq'}, dimensions={0} | all-to-all | bytes 1048576 | tf_op jit(solution)/shard_map/all_to_all | solution.py:48
  168.2 137.7 %all-gather.2.cloned.1.call-done = bf16[16,128,2048]{2,1,0:T(8,128)(2,1)} async-done(((bf16[1,128,2048]{2,1,0:T(8,128)(2,1)}), bf16[16,128,2048]{2,1,0:T(8,128)(2,1)}) %all-gather.2.cloned.1.call-update) | async-done | bytes 8388624 | tf_op jit(solution)/shard_map/all_gather | solution.py:51
  305.9 6.8 %fusion.39 = bf16[16,128,2,128]{3,1,2,0:T(8,128)(2,1)} fusion(bf16[16,128,2048]{2,1,0:T(8,128)(2,1)} %all-gather.2.cloned.1.call-done, bf16[2,2048,128]{2,1,0:T(8,128)(2,1)S(1)} %copy-done), kind=kOutput, calls=%fused_computation.31 | convolution fusion | flops 2148007936 | bytes 10485760 | tf_op jit(solution)/shard_map/btd,kdc->btkc/dot_general | solution.py:49
  312.7 4.3 all-to-all-start.4
  318.1 25.2 %all-to-all-done.4 = bf16[16,128,2,128]{3,1,2,0:T(8,128)(2,1)S(1)} async-done(((bf16[16,128,2,128]{3,1,2,0:T(8,128)(2,1)}), bf16[16,128,2,128]{3,1,2,0:T(8,128)(2,1)S(1)}, u32[]{:S(2)}, u32[]{:S(2)}) %all-to-all-start.4) | async-done | bytes 1048608 | tf_op jit(solution)/shard_map/all_to_all | solution.py:57
  343.3 13.0 %all-to-all-start.6 = ((bf16[32,2,512]{2,1,0:T(2,128)(2,1)}), bf16[32,2,512]{2,1,0:T(2,128)(2,1)S(1)}, u32[]{:S(2)}, u32[]{:S(2)}) async-start(bf16[32,2,512]{2,1,0:T(2,128)(2,1)} %reshape.128), calls=%async_computation.6 | async-start | bytes 131072 | tf_op jit(solution)/shard_map/all_to_all | solution.py:65
  357.0 9.5 %copy.54 = bf16[1,128,2,2048]{1,2,0,3:T(2,128)(2,1)} copy(bf16[1,128,2,2048]{1,3,2,0:T(8,128)(2,1)S(1)} %bitcast.112) | data formatting | bytes 2097152 | tf_op jit(solution)/shard_map/all_to_all | solution.py:57
  366.5 8.3 %all-to-all-start.5 = ((bf16[1,128,2,2048]{1,2,0,3:T(2,128)(2,1)}), bf16[1,128,2,2048]{1,2,0,3:T(2,128)(2,1)S(1)}, u32[]{:S(2)}, u32[]{:S(2)}) async-start(bf16[1,128,2,2048]{1,2,0,3:T(2,128)(2,1)} %copy.54), calls=%async_computation.5 | async-start | bytes 2097152 | tf_op jit(solution)/shard_map/all_to_all | solution.py:56
  375.6 27.1 %all-to-all-done.5 = bf16[1,128,2,2048]{1,2,0,3:T(2,128)(2,1)S(1)} async-done(((bf16[1,128,2,2048]{1,2,0,3:T(2,128)(2,1)}), bf16[1,128,2,2048]{1,2,0,3:T(2,128)(2,1)S(1)}, u32[]{:S(2)}, u32[]{:S(2)}) %all-to-all-start.5) | async-done | bytes 1048608 | tf_op jit(solution)/shard_map/all_to_all | solution.py:56
  403.1 3.4 fusion.33
  406.5 2.7 fusion.34
  411.3 12.6 %all_to_all.133 = bf16[32,2,512]{2,1,0:T(2,128)(2,1)S(1)} all-to-all(bf16[32,2,512]{2,1,0:T(2,128)(2,1)S(1)} %reshape.130), channel_id=1, replica_groups=mesh['doc'=16,'seq'=32] {'seq'}, dimensions={0} | all-to-all | bytes 131072 | tf_op jit(solution)/shard_map/all_to_all | solution.py:67
  (63 shorter events, 65.4 us)
Async XLA Ops:
  7.2 298.8 %copy-start = (bf16[2,2048,128]{2,1,0:T(8,128)(2,1)S(1)}, bf16[2,2048,128]{2,1,0:T(8,128)(2,1)}, u32[]{:S(2)}) copy-start(bf16[2,2048,128]{2,1,0:T(8,128)(2,1)} %param.13) | copy-start | bytes 3145732
  9.3 29.6 %all-to-all-start = ((bf16[128,32,64]{0,2,1:T(8,128)(2,1)}), bf16[128,32,64]{0,2,1:T(8,128)(2,1)S(1)}, u32[]{:S(2)}, u32[]{:S(2)}) async-start(bf16[128,32,64]{0,2,1:T(8,128)(2,1)} %bitcast), calls=%async_computation | async-start | bytes 1048576 | tf_op jit(solution)/shard_map/all_to_all | solution.py:43
  38.9 22.2 %all-to-all-start.1 = ((bf16[128,32,64]{0,2,1:T(8,128)(2,1)}), bf16[128,32,64]{0,2,1:T(8,128)(2,1)S(1)}, u32[]{:S(2)}, u32[]{:S(2)}) async-start(bf16[128,32,64]{0,2,1:T(8,128)(2,1)} %bitcast.2), calls=%async_computation.1 | async-start | bytes 1048576 | tf_op jit(solution)/shard_map/all_to_all | solution.py:44
  61.1 21.9 %all-to-all-start.2 = ((bf16[128,32,64]{0,2,1:T(8,128)(2,1)}), bf16[128,32,64]{0,2,1:T(8,128)(2,1)S(1)}, u32[]{:S(2)}, u32[]{:S(2)}) async-start(bf16[128,32,64]{0,2,1:T(8,128)(2,1)} %bitcast.4), calls=%async_computation.2 | async-start | bytes 1048576 | tf_op jit(solution)/shard_map/all_to_all | solution.py:45
  66.0 240.0 %all-gather.2.cloned.1.call-start = ((), (), s32[]{:S(2)}) async-start(), calls=%async_computation.8 | async-start | bytes 8912896 | tf_op jit(solution)/shard_map/all_gather | solution.py:51
  168.2 148.8 %copy-start.1 = (bf16[1,16,2048]{2,1,0:T(8,128)(2,1)S(1)}, bf16[1,16,2048]{2,1,0:T(8,128)(2,1)}, u32[]{:S(2)}) copy-start(bf16[1,16,2048]{2,1,0:T(8,128)(2,1)} %param.11) | copy-start | bytes 196612
  312.7 30.6 %all-to-all-start.4 = ((bf16[16,128,2,128]{3,1,2,0:T(8,128)(2,1)}), bf16[16,128,2,128]{3,1,2,0:T(8,128)(2,1)S(1)}, u32[]{:S(2)}, u32[]{:S(2)}) async-start(bf16[16,128,2,128]{3,1,2,0:T(8,128)(2,1)} %fusion.39), calls=%async_computation.4 | async-start | bytes 2097152 | tf_op jit(solution)/shard_map/all_to_all | solution.py:57
  343.3 23.1 %all-to-all-start.6 = ((bf16[32,2,512]{2,1,0:T(2,128)(2,1)}), bf16[32,2,512]{2,1,0:T(2,128)(2,1)S(1)}, u32[]{:S(2)}, u32[]{:S(2)}) async-start(bf16[32,2,512]{2,1,0:T(2,128)(2,1)} %reshape.128), calls=%async_computation.6 | async-start | bytes 131072 | tf_op jit(solution)/shard_map/all_to_all | solution.py:65
  366.5 36.2 %all-to-all-start.5 = ((bf16[1,128,2,2048]{1,2,0,3:T(2,128)(2,1)}), bf16[1,128,2,2048]{1,2,0,3:T(2,128)(2,1)S(1)}, u32[]{:S(2)}, u32[]{:S(2)}) async-start(bf16[1,128,2,2048]{1,2,0,3:T(2,128)(2,1)} %copy.54), calls=%async_computation.5 | async-start | bytes 2097152 | tf_op jit(solution)/shard_map/all_to_all | solution.py:56
Sparse Core Ops, SparseCore 0:
  168.3 137.5 all-gather.1
where the time goes:
time: 433 us; the launch traced here: 432 us
  waiting for transfers between devices  235 us (54%)
  matrix products  50.5 us (12%)
  starting transfers between devices  48.4 us (11%)
  blocking collectives  33.4 us (8%)
  other arithmetic  25.1 us (6%)
  local copies, waits for them, and re-layouts  24.8 us (6%)
  between operations  14.9 us (3%)
    all_gather x1, waiting for transfers between devices, shards(): lax.all_gather(encoder_out[None], 'doc', axis=0, tiled=True)  138 us
    all_to_all x1, waiting for transfers between devices, shards(): lax.all_to_all(lax.all_to_all(memory_rows, 'doc', split_axis=0, concat_ax...  27.1 us
    all_to_all x1, waiting for transfers between devices, shards(): lax.all_to_all(memory_rows, 'doc', split_axis=0, concat_axis=3, tiled=True)  25.2 us
    dot_general x9, matrix products, one_block(): jnp.einsum('hqk,khd->qhd', weights.astype(jnp.bfloat16), value_heads, pre...  22.1 us
    dot_general x9, matrix products, one_block(): jnp.einsum('qhd,khd->hqk', query_block, key_heads, preferred_element_type...  21.5 us
    all_to_all x1, blocking collectives, shards(): lax.all_to_all(context, 'seq', split_axis=0, concat_axis=1, tiled=True)  20.8 us
    reduce_sum x9, other arithmetic, one_block(): denominator = jnp.sum(weights, axis=-1)  19.9 us
    all_to_all x1, waiting for transfers between devices, shards(): lax.all_to_all(enc_key[0], 'seq', split_axis=1, concat_axis=0, tiled=True)  15 us
  transfers between devices with their start and end apart: 7, of which 6 were waited for; matrix products, arithmetic and copies ran while one was open for 4% of the time, Pallas kernels for 0%

commit v1 on v0

--- a/solution.py
+++ b/solution.py
@@ -48,7 +48,10 @@
     encoder_out = lax.all_to_all(context, "seq", split_axis=0, concat_axis=1, tiled=True)
     made = jnp.einsum(
         "btd,kdc->btkc",
-        lax.all_gather(encoder_out[None], "doc", axis=0, tiled=True),
+        jnp.concatenate(
+            lax.all_to_all(jnp.stack([encoder_out[None]] * lax.axis_size("doc")), "doc", 0, 0),
+            axis=0,
+        ),
         w_memory,
         preferred_element_type=jnp.float32,
     )

time: 433 us -> 465 us (1.074)
  blocking collectives: 33.4 us -> 215 us
  waiting for transfers between devices: 235 us -> 108 us
  between operations: 14.9 us -> 1.51 us
    all_to_all x1, blocking collectives: 12.6 us -> 194 us  [shards(): lax.all_to_all(jnp.stack([encoder_out[None]] * lax.axis_size('doc')), 'do...]
    all_gather x1 -> x0, waiting for transfers between devices: 138 us -> none  [shards(): lax.all_gather(encoder_out[None], 'doc', axis=0, tiled=True)]
    all_to_all x0 -> x1, waiting for transfers between devices: none -> 7.42 us  [shards(): lax.all_to_all(answer, 'seq', split_axis=0, concat_axis=1, tiled=True)]
    all_to_all x2, local copies, waits for them, and re-layouts: 10.2 us -> 4.92 us  [shards(): lax.all_to_all(memory_rows, 'doc', split_axis=0, concat_axis=3, tiled=True)]
    all_to_all x0 -> x1, starting transfers between devices: none -> 4.71 us  [shards(): lax.all_to_all(answer, 'seq', split_axis=0, concat_axis=1, tiled=True)]
  transfers between devices with their start and end apart: 7 -> 7, of which waited for: 6 -> 7; matrix products, arithmetic and copies ran while one was open for 4% -> 3% of each run, Pallas kernels for 0% -> 0%
where the time goes in v1:
time: 465 us; the launch traced here: 464 us
  blocking collectives  215 us (46%)
  waiting for transfers between devices  108 us (23%)
  matrix products  47.1 us (10%)
  starting transfers between devices  46.5 us (10%)
  other arithmetic  25.1 us (5%)
  local copies, waits for them, and re-layouts  21.4 us (5%)
    all_to_all x1, blocking collectives, shards(): lax.all_to_all(jnp.stack([encoder_out[None]] * lax.axis_size('doc')), 'do...  194 us
    all_to_all x1, waiting for transfers between devices, shards(): lax.all_to_all(lax.all_to_all(memory_rows, 'doc', split_axis=0, concat_ax...  27.3 us
    all_to_all x1, waiting for transfers between devices, shards(): lax.all_to_all(memory_rows, 'doc', split_axis=0, concat_axis=3, tiled=True)  24.9 us
    dot_general x9, matrix products, one_block(): jnp.einsum('hqk,khd->qhd', weights.astype(jnp.bfloat16), value_heads, pre...  22.1 us
    dot_general x9, matrix products, one_block(): jnp.einsum('qhd,khd->hqk', query_block, key_heads, preferred_element_type...  21.6 us
    all_to_all x1, blocking collectives, shards(): lax.all_to_all(context, 'seq', split_axis=0, concat_axis=1, tiled=True)  20.7 us
    reduce_sum x9, other arithmetic, one_block(): denominator = jnp.sum(weights, axis=-1)  19.9 us
    all_to_all x1, waiting for transfers between devices, shards(): lax.all_to_all(enc_key[0], 'seq', split_axis=1, concat_axis=0, tiled=True)  15 us
  transfers between devices with their start and end apart: 7, of which 7 were waited for; matrix products, arithmetic and copies ran while one was open for 3% of the time, Pallas kernels for 0%

profile of v1, /device:TPU:1, one launch (start us, length us, event | category | flops | bytes accessed | tf_op | source)
XLA Modules:
  0.0 464.0 jit_solution(15954675010087482746)
XLA Ops:
  2.8 12.9 %all-to-all-start = ((bf16[128,32,64]{0,2,1:T(8,128)(2,1)}), bf16[128,32,64]{0,2,1:T(8,128)(2,1)S(1)}, u32[]{:S(2)}, u32[]{:S(2)}) async-start(bf16[128,32,64]{0,2,1:T(8,128)(2,1)} %bitcast), calls=%async_computation | async-start | bytes 1048576 | tf_op jit(solution)/shard_map/all_to_all | solution.py:43
  17.7 14.7 %all-to-all-done = bf16[128,32,64]{0,2,1:T(8,128)(2,1)S(1)} async-done(((bf16[128,32,64]{0,2,1:T(8,128)(2,1)}), bf16[128,32,64]{0,2,1:T(8,128)(2,1)S(1)}, u32[]{:S(2)}, u32[]{:S(2)}) %all-to-all-start) | async-done | bytes 524320 | tf_op jit(solution)/shard_map/all_to_all | solution.py:43
  32.4 5.1 %all-to-all-start.1 = ((bf16[128,32,64]{0,2,1:T(8,128)(2,1)}), bf16[128,32,64]{0,2,1:T(8,128)(2,1)S(1)}, u32[]{:S(2)}, u32[]{:S(2)}) async-start(bf16[128,32,64]{0,2,1:T(8,128)(2,1)} %bitcast.2), calls=%async_computation.1 | async-start | bytes 1048576 | tf_op jit(solution)/shard_map/all_to_all | solution.py:44
  39.5 15.0 %all-to-all-done.1 = bf16[128,32,64]{0,2,1:T(8,128)(2,1)S(1)} async-done(((bf16[128,32,64]{0,2,1:T(8,128)(2,1)}), bf16[128,32,64]{0,2,1:T(8,128)(2,1)S(1)}, u32[]{:S(2)}, u32[]{:S(2)}) %all-to-all-start.1) | async-done | bytes 524320 | tf_op jit(solution)/shard_map/all_to_all | solution.py:44
  54.6 4.8 %all-to-all-start.2 = ((bf16[128,32,64]{0,2,1:T(8,128)(2,1)}), bf16[128,32,64]{0,2,1:T(8,128)(2,1)S(1)}, u32[]{:S(2)}, u32[]{:S(2)}) async-start(bf16[128,32,64]{0,2,1:T(8,128)(2,1)} %bitcast.4), calls=%async_computation.2 | async-start | bytes 1048576 | tf_op jit(solution)/shard_map/all_to_all | solution.py:45
  61.6 14.9 %all-to-all-done.2 = bf16[128,32,64]{0,2,1:T(8,128)(2,1)S(1)} async-done(((bf16[128,32,64]{0,2,1:T(8,128)(2,1)}), bf16[128,32,64]{0,2,1:T(8,128)(2,1)S(1)}, u32[]{:S(2)}, u32[]{:S(2)}) %all-to-all-start.2) | async-done | bytes 524320 | tf_op jit(solution)/shard_map/all_to_all | solution.py:45
  77.1 60.9 %while.3 = (s32[]{:T(128)}, bf16[8,512,1,64]{1,3,2,0:T(8,128)(2,1)}, bf16[8,512,1,64]{1,3,2,0:T(8,128)(2,1)}, bf16[4096,1,64]{0,2,1:T(8,128)(2,1)S(1)}, bf16[409...) while((s32[]{:T(128)}, bf16[8,512,1,64]{1,3,2,0:T(8,128)(2,1)}, ...), condition=%wide.region_3.4_spmd.clone, body=%wide.region_0.3_spmd.clone.sunk | while | flops 560008192 | bytes 26373200 | solution.py:36
  105.0 2.5 fusion.68
  120.2 2.5 fusion.68
  135.4 2.5 fusion.68
  139.9 20.7 %all_to_all.137 = bf16[32,128,64]{1,2,0:T(8,128)(2,1)S(1)} all-to-all(bf16[32,128,64]{1,2,0:T(8,128)(2,1)S(1)} %copy.53), channel_id=1, replica_groups=mesh['doc'=16,'seq'=32] {'seq'}, dimensions={0} | all-to-all | bytes 1048576 | tf_op jit(solution)/shard_map/all_to_all | solution.py:48
  161.9 193.9 %all_to_all.138 = bf16[16,1,128,2048]{3,2,1,0:T(8,128)(2,1)S(1)} all-to-all(bf16[16,1,128,2048]{3,2,1,0:T(8,128)(2,1)S(1)} %stack.3), channel_id=1, replica_groups=mesh['doc'=16,'seq'=32] {'doc'}, dimensions={0} | all-to-all | bytes 16777216 | tf_op jit(solution)/shard_map/all_to_all | solution.py:52
  355.8 3.4 fusion.39
  359.2 4.3 all-to-all-start.5
  364.5 24.9 %all-to-all-done.5 = bf16[16,128,2,128]{3,1,2,0:T(8,128)(2,1)S(1)} async-done(((bf16[16,128,2,128]{3,1,2,0:T(8,128)(2,1)}), bf16[16,128,2,128]{3,1,2,0:T(8,128)(2,1)S(1)}, u32[]{:S(2)}, u32[]{:S(2)}) %all-to-all-start.5) | async-done | bytes 1048608 | tf_op jit(solution)/shard_map/all_to_all | solution.py:60
  389.4 9.8 %all-to-all-start.7 = ((bf16[32,2,512]{2,1,0:T(2,128)(2,1)}), bf16[32,2,512]{2,1,0:T(2,128)(2,1)S(1)}, u32[]{:S(2)}, u32[]{:S(2)}) async-start(bf16[32,2,512]{2,1,0:T(2,128)(2,1)} %reshape.137), calls=%async_computation.7 | async-start | bytes 131072 | tf_op jit(solution)/shard_map/all_to_all | solution.py:68
  400.5 3.6 copy.56
  404.2 3.4 all-to-all-done.7
  407.6 4.9 %all-to-all-start.6 = ((bf16[1,128,2,2048]{1,2,0,3:T(2,128)(2,1)}), bf16[1,128,2,2048]{1,2,0,3:T(2,128)(2,1)S(1)}, u32[]{:S(2)}, u32[]{:S(2)}) async-start(bf16[1,128,2,2048]{1,2,0,3:T(2,128)(2,1)} %copy.56), calls=%async_computation.6 | async-start | bytes 2097152 | tf_op jit(solution)/shard_map/all_to_all | solution.py:59
  413.2 27.3 %all-to-all-done.6 = bf16[1,128,2,2048]{1,2,0,3:T(2,128)(2,1)S(1)} async-done(((bf16[1,128,2,2048]{1,2,0,3:T(2,128)(2,1)}), bf16[1,128,2,2048]{1,2,0,3:T(2,128)(2,1)S(1)}, u32[]{:S(2)}, u32[]{:S(2)}) %all-to-all-start.6) | async-done | bytes 1048608 | tf_op jit(solution)/shard_map/all_to_all | solution.py:59
  441.0 3.4 fusion.33
  444.4 2.7 fusion.34
  449.9 4.7 %all-to-all-start.8 = ((bf16[32,2,512]{2,1,0:T(2,128)(2,1)}), bf16[32,2,512]{2,1,0:T(2,128)(2,1)S(1)}, u32[]{:S(2)}, u32[]{:S(2)}) async-start(bf16[32,2,512]{2,1,0:T(2,128)(2,1)} %reshape.139), calls=%async_computation.8 | async-start | bytes 131072 | tf_op jit(solution)/shard_map/all_to_all | solution.py:70
  455.6 7.4 %all-to-all-done.8 = bf16[32,2,512]{2,1,0:T(2,128)(2,1)S(1)} async-done(((bf16[32,2,512]{2,1,0:T(2,128)(2,1)}), bf16[32,2,512]{2,1,0:T(2,128)(2,1)S(1)}, u32[]{:S(2)}, u32[]{:S(2)}) %all-to-all-start.8) | async-done | bytes 65568 | tf_op jit(solution)/shard_map/all_to_all | solution.py:70
  (64 shorter events, 72.9 us)
Async XLA Ops:
  0.6 355.1 %copy-start = (bf16[2,2048,128]{2,1,0:T(8,128)(2,1)S(1)}, bf16[2,2048,128]{2,1,0:T(8,128)(2,1)}, u32[]{:S(2)}) copy-start(bf16[2,2048,128]{2,1,0:T(8,128)(2,1)} %param.13) | copy-start | bytes 3145732
  2.8 29.6 %all-to-all-start = ((bf16[128,32,64]{0,2,1:T(8,128)(2,1)}), bf16[128,32,64]{0,2,1:T(8,128)(2,1)S(1)}, u32[]{:S(2)}, u32[]{:S(2)}) async-start(bf16[128,32,64]{0,2,1:T(8,128)(2,1)} %bitcast), calls=%async_computation | async-start | bytes 1048576 | tf_op jit(solution)/shard_map/all_to_all | solution.py:43
  32.4 22.2 %all-to-all-start.1 = ((bf16[128,32,64]{0,2,1:T(8,128)(2,1)}), bf16[128,32,64]{0,2,1:T(8,128)(2,1)S(1)}, u32[]{:S(2)}, u32[]{:S(2)}) async-start(bf16[128,32,64]{0,2,1:T(8,128)(2,1)} %bitcast.2), calls=%async_computation.1 | async-start | bytes 1048576 | tf_op jit(solution)/shard_map/all_to_all | solution.py:44
  54.6 21.9 %all-to-all-start.2 = ((bf16[128,32,64]{0,2,1:T(8,128)(2,1)}), bf16[128,32,64]{0,2,1:T(8,128)(2,1)S(1)}, u32[]{:S(2)}, u32[]{:S(2)}) async-start(bf16[128,32,64]{0,2,1:T(8,128)(2,1)} %bitcast.4), calls=%async_computation.2 | async-start | bytes 1048576 | tf_op jit(solution)/shard_map/all_to_all | solution.py:45
  355.8 7.7 %copy-start.1 = (bf16[1,16,2048]{2,1,0:T(8,128)(2,1)S(1)}, bf16[1,16,2048]{2,1,0:T(8,128)(2,1)}, u32[]{:S(2)}) copy-start(bf16[1,16,2048]{2,1,0:T(8,128)(2,1)} %param.11) | copy-start | bytes 196612
  359.2 30.2 %all-to-all-start.5 = ((bf16[16,128,2,128]{3,1,2,0:T(8,128)(2,1)}), bf16[16,128,2,128]{3,1,2,0:T(8,128)(2,1)S(1)}, u32[]{:S(2)}, u32[]{:S(2)}) async-start(bf16[16,128,2,128]{3,1,2,0:T(8,128)(2,1)} %fusion.39), calls=%async_computation.5 | async-start | bytes 2097152 | tf_op jit(solution)/shard_map/all_to_all | solution.py:60
  389.4 18.1 %all-to-all-start.7 = ((bf16[32,2,512]{2,1,0:T(2,128)(2,1)}), bf16[32,2,512]{2,1,0:T(2,128)(2,1)S(1)}, u32[]{:S(2)}, u32[]{:S(2)}) async-start(bf16[32,2,512]{2,1,0:T(2,128)(2,1)} %reshape.137), calls=%async_computation.7 | async-start | bytes 131072 | tf_op jit(solution)/shard_map/all_to_all | solution.py:68
  407.6 33.0 %all-to-all-start.6 = ((bf16[1,128,2,2048]{1,2,0,3:T(2,128)(2,1)}), bf16[1,128,2,2048]{1,2,0,3:T(2,128)(2,1)S(1)}, u32[]{:S(2)}, u32[]{:S(2)}) async-start(bf16[1,128,2,2048]{1,2,0,3:T(2,128)(2,1)} %copy.56), calls=%async_computation.6 | async-start | bytes 2097152 | tf_op jit(solution)/shard_map/all_to_all | solution.py:59
  449.9 13.1 %all-to-all-start.8 = ((bf16[32,2,512]{2,1,0:T(2,128)(2,1)}), bf16[32,2,512]{2,1,0:T(2,128)(2,1)S(1)}, u32[]{:S(2)}, u32[]{:S(2)}) async-start(bf16[32,2,512]{2,1,0:T(2,128)(2,1)} %reshape.139), calls=%async_computation.8 | async-start | bytes 131072 | tf_op jit(solution)/shard_map/all_to_all | solution.py:70
